TPU v7x, 32 devices: a whole 2x2x4 slice. The times are simulated.
32 devices in a mesh: section: 2 (over x), head: 4 (over y, core), tok: 4 (over z).
Axes of the slice: x: 2, y: 2, z: 4, core: 2. Of those that a mesh axis runs over, the one named last changes fastest.
Arguments:
- held_cotangents: bfloat16 [2, 2, 512, 2560], P('section', None, 'tok', 'head'), may hold values from -6 to 6
- entering_adjoint: bfloat16 [512, 2560], P('tok', 'head'), may hold values from -6 to 6
- saved_queries: bfloat16 [2, 512, 2560], P('section', 'tok', 'head'), may hold values from -1024 to 1024
- saved_keys: bfloat16 [2, 512, 2560], P('section', 'tok', 'head'), may hold values from -20 to 20
- value_weight: bfloat16 [2, 2560, 2560], P('section', None, 'head'), may hold values from -0.125 to 0.125
- out_weight: bfloat16 [2, 2560, 2560], P('section', 'tok', 'head'), may hold values from -0.125 to 0.125
- block_gate: float32 [2, 2560], P('section'), may hold values from -3 to 3
- time_gate: float32 [32, 2560], replicated, may hold values from -3 to 3
- timestep: int32 [1], replicated, may hold values from 0 to 31
Outputs:
- passed: bfloat16 [2, 2, 512, 2560], P('section', None, 'tok', 'head')
All inputs are finite; a program needn't handle non-finite values.
Results may differ from a plain program's by a relative error of at most 0.0085.
Values may be sent and summed in bfloat16 or wider, within the bound.
No kernel may reach another device: no remote copies, remote signals or barrier semaphores. Data moves between devices by JAX's collectives and lax.ppermute only.
A program may use at most 64 MiB of HBM per device.

v0:
```python
import jax
import jax.numpy as jnp
from jax import lax
from jax.sharding import PartitionSpec as P

HD = 128
GUIDE = 3.0


def combined_all(part, axis, combine):
    gathered = jax.tree.map(lambda a: lax.all_gather(a, axis), part)

    def take(source):
        return jax.tree.map(lambda a: lax.dynamic_index_in_dim(a, source, 0, False), gathered)

    return lax.fori_loop(
        1, lax.axis_size(axis), lambda source, state: combine(state, take(source)), take(0)
    )


def shifted(value, axis, steps):
    count = lax.axis_size(axis)
    leading, last = (max(0, -steps), min(count, count - steps))
    return lax.ppermute(value, axis, [(source, source + steps) for source in range(leading, last)])


def merge_stats(earlier, latter):
    row_top = jnp.maximum(earlier[0], latter[0])
    total_sum = earlier[1] * jnp.exp(earlier[0] - row_top) + latter[1] * jnp.exp(
        latter[0] - row_top
    )
    return (row_top, total_sum)


def body(
    held_cotangents,
    entering_adjoint,
    saved_queries,
    saved_keys,
    value_weight,
    out_weight,
    block_gate,
    time_gate,
    timestep,
):
    steps_index = jnp.arange(time_gate.shape[0])
    time_row = jnp.sum(
        jnp.where((steps_index == timestep[0])[:, None], time_gate, jnp.zeros_like(time_gate)),
        axis=0,
    )
    gate_row = block_gate[0] + time_row
    whole_cot = lax.all_gather(held_cotangents[0], "head", axis=2, tiled=True)
    scaled = (whole_cot.astype(jnp.float32) * gate_row).astype(jnp.bfloat16)
    out_full = lax.all_gather(out_weight[0], "tok", axis=0, tiled=True)
    attn_grad = jnp.einsum(
        "btd,dk->btk", scaled, out_full, preferred_element_type=jnp.float32
    ).astype(jnp.bfloat16)
    rows_here = saved_queries.shape[1]
    groups_here = saved_queries.shape[2] // HD
    score_scale = HD ** (-0.5)
    normal_grad = attn_grad[0]
    query_all = lax.all_gather(saved_queries[0], "tok", axis=0, tiled=True)
    total_rows = query_all.shape[0]
    shards = total_rows // rows_here
    key_heads = saved_keys[0].reshape(rows_here, groups_here, HD)
    scores = (
        jnp.einsum(
            "ihe,jhe->hij",
            query_all.reshape(total_rows, groups_here, HD),
            key_heads,
            preferred_element_type=jnp.float32,
        )
        * score_scale
    )
    row_top = jnp.max(scores, axis=2)
    partial_total = jnp.sum(jnp.exp(scores - row_top[:, :, None]), axis=2)
    top_all, total_all = combined_all((row_top, partial_total), "tok", merge_stats)
    log_total = top_all + jnp.log(total_all)
    weights = jnp.exp(scores - log_total[:, :, None]).astype(jnp.bfloat16)
    grad_all = lax.all_gather(normal_grad, "tok", axis=0, tiled=True)
    blocked = jnp.einsum(
        "hbij,bihe->bjhe",
        weights.reshape(groups_here, shards, rows_here, rows_here),
        grad_all.reshape(shards, rows_here, groups_here, HD),
        preferred_element_type=jnp.float32,
    )
    blocked = lax.optimization_barrier(blocked.astype(jnp.bfloat16))
    value_grad = (
        jnp.sum(blocked.astype(jnp.float32), axis=0)
        .reshape(rows_here, groups_here * HD)
        .astype(jnp.bfloat16)
    )
    stacked = jnp.stack([value_grad, attn_grad[1]])
    partial_back = jnp.einsum(
        "btk,dk->btd", stacked, value_weight[0], preferred_element_type=jnp.float32
    )
    back_sum = lax.psum_scatter(
        partial_back.astype(jnp.bfloat16), "head", scatter_dimension=2, tiled=True
    ).astype(jnp.float32)
    block_cot = (held_cotangents[0].astype(jnp.float32) + back_sum).astype(jnp.bfloat16)
    passed_on = shifted(block_cot, "section", -1)
    entering_full = entering_adjoint.astype(jnp.float32)
    fresh_rows = jnp.stack([(1.0 + GUIDE) * entering_full, -GUIDE * entering_full]).astype(
        jnp.bfloat16
    )
    is_last = lax.axis_index("section") == lax.axis_size("section") - 1
    return jnp.where(is_last, fresh_rows, passed_on)[None]


def solution(mesh):
    return jax.shard_map(
        body,
        mesh=mesh,
        in_specs=(
            P("section", None, "tok", "head"),
            P("tok", "head"),
            P("section", "tok", "head"),
            P("section", "tok", "head"),
            P("section", None, "head"),
            P("section", "tok", "head"),
            P("section", None),
            P(),
            P(),
        ),
        out_specs=P("section", None, "tok", "head"),
        check_vma=False,
    )
```

profile of v0, /device:TPU:0, one launch (start us, length us, event | category | flops | bytes accessed | tf_op | source)
XLA Modules:
  0.0 187.7 jit_solution(18396355772146746361)
XLA Ops:
  8.7 1.7 copy.22
  10.4 1.1 copy.23
  11.6 1.1 select_reduce_fusion
  12.7 19.1 %all-gather.3 = bf16[1,512,640]{1,2,0:T(8,128)(2,1)S(1)} all-gather(bf16[1,128,640]{1,2,0:T(8,128)(2,1)} %copy.22), channel_id=5, replica_groups=mesh['section'=2,'head'=4,'tok'=4] {'tok'}, dimensions={1}, use_global_device_ids=true | all-gather | bytes 819200 | tf_op jit(solution)/shard_map/all_gather | solution.py:62
  32.4 13.4 %all-gather.6 = f32[4,5,512]{2,1,0:T(8,128)S(1)} all-gather(f32[1,5,512]{2,1,0:T(8,128)S(1)} %bitcast.70), channel_id=6, replica_groups=mesh['section'=2,'head'=4,'tok'=4] {'tok'}, dimensions={0}, use_global_device_ids=true | all-gather | bytes 51200 | tf_op jit(solution)/shard_map/all_gather | solution.py:11
  46.6 14.1 %all-gather.7 = f32[4,5,512]{2,1,0:T(8,128)S(1)} all-gather(f32[1,5,512]{2,1,0:T(8,128)S(1)} %bitcast.71), channel_id=7, replica_groups=mesh['section'=2,'head'=4,'tok'=4] {'tok'}, dimensions={0}, use_global_device_ids=true | all-gather | bytes 51200 | tf_op jit(solution)/shard_map/all_gather | solution.py:11
  60.9 2.6 %exponential_convert_fusion = bf16[5,512,128]{2,1,0:T(8,128)(2,1)} fusion(f32[5,512,128]{2,1,0:T(8,128)} %copy-done.1, f32[5,512]{1,0:T(8,128)S(1)} %log_add_fusion), kind=kLoop, calls=%fused_computation.15 | loop fusion | flops 655360 | bytes 1976320 | tf_op jit(solution)/shard_map/convert_element_type | solution.py:79
  63.4 34.6 %all-gather.13.cloned.1.call-done = bf16[1,2560,640]{2,1,0:T(8,128)(2,1)} async-done(((bf16[1,640,640]{2,1,0:T(8,128)(2,1)}), bf16[1,2560,640]{2,1,0:T(8,128)(2,1)}) %all-gather.13.cloned.1.call-update) | async-done | bytes 3276816 | tf_op jit(solution)/shard_map/all_gather | solution.py:54
  98.0 3.5 %fusion.10 = bf16[2,128,640]{2,1,0:T(8,128)(2,1)S(1)} fusion(bf16[1,2560,640]{2,1,0:T(8,128)(2,1)} %all-gather.13.cloned.1.call-done, bf16[1,2,128,2560]{3,2,1,0:T(8,128)(2,1)} %all-gather.11.cloned.1.call-done, f32[2560]{0:T(1024)S(1)} %add.62), kind=kOutput, calls=%fused_computation.19 | convolution fusion | flops 840990720 | bytes 4925440 | tf_op jit(solution)/shard_map/btd,dk->btk/dot_general | solution.py:55
  102.3 17.6 %all-gather.2 = bf16[1,512,640]{2,1,0:T(8,128)(2,1)} all-gather(bf16[1,128,640]{2,1,0:T(8,128)(2,1)S(1)} %get-tuple-element.152), channel_id=4, replica_groups=mesh['section'=2,'head'=4,'tok'=4] {'tok'}, dimensions={1}, use_global_device_ids=true | all-gather | bytes 819200 | tf_op jit(solution)/shard_map/all_gather | solution.py:80
  119.9 2.5 %reshape.61 = bf16[4,128,5,128]{3,2,1,0:T(8,128)(2,1)} reshape(bf16[1,512,640]{2,1,0:T(8,128)(2,1)} %all-gather.2) | data formatting | bytes 1310720 | tf_op jit(solution)/shard_map/reshape | solution.py:84
  122.4 2.7 %fusion.9 = bf16[4,128,5,128]{1,3,2,0:T(8,128)(2,1)} fusion(bf16[4,128,5,128]{3,2,1,0:T(8,128)(2,1)} %reshape.61, bf16[5,4,128,128]{3,2,1,0:T(8,128)(2,1)} %bitcast.66), kind=kOutput, calls=%fused_computation.18 | convolution fusion | flops 84213760 | bytes 1966080 | tf_op jit(solution)/shard_map/hbij,bihe->bjhe/dot_general | solution.py:81
  125.1 1.2 reduce_sum.32
  126.3 0.8 copy.28
  127.1 3.3 %convolution_convert_fusion = bf16[2,128,2560]{2,1,0:T(8,128)(2,1)} fusion(bf16[1,2560,640]{2,1,0:T(8,128)(2,1)S(1)} %copy-done, bf16[1,128,640]{2,1,0:T(8,128)(2,1)} %get-tuple-element.153, bf16[1,128,640]{2,1,0:T(8,128)(2,1)} %copy.28), kind=kOutput, calls=%fused_computation.5 | convolution fusion | flops 839680000 | bytes 4915200 | tf_op jit(solution)/shard_map/btk,dk->btd/dot_general | solution.py:94
  130.4 4.3 %copy.33 = bf16[2,128,2560]{1,0,2:T(2,128)(2,1)} copy(bf16[2,128,2560]{2,1,0:T(8,128)(2,1)} %convolution_convert_fusion) | data formatting | bytes 2621440
  134.7 2.6 %copy.41 = bf16[320,8,2,128]{3,1,2,0:T(8,128)(2,1)} copy(bf16[320,8,2,128]{3,2,1,0:T(2,128)(2,1)} %bitcast.64) | data formatting | bytes 2621440
  137.3 25.1 %reduce-scatter.4.cloned.1.call-done = bf16[640,256]{1,0:T(8,128)(2,1)} async-done(((bf16[2560,256]{1,0:T(8,128)(2,1)}), bf16[640,256]{1,0:T(8,128)(2,1)}) %reduce-scatter.4.cloned.1.call-update) | async-done | bytes 327696
  162.4 1.8 reshape.63
  164.1 1.9 %copy.34 = bf16[2,128,640]{2,1,0:T(8,128)(2,1)} copy(bf16[2,128,640]{1,0,2:T(2,128)(2,1)} %bitcast.67) | data formatting | bytes 655360
  166.1 1.9 fusion.15
  167.9 1.3 collective-permute-start
  169.3 10.1 %collective-permute-done = bf16[2,128,640]{2,1,0:T(8,128)(2,1)} collective-permute-done((bf16[2,128,640]{2,1,0:T(8,128)(2,1)}, bf16[2,128,640]{2,1,0:T(8,128)(2,1)}, u32[]{:S(2)}, u32[]{:S(2)}) %collective-permute-start) | collective-permute-done | bytes 327712 | tf_op jit(solution)/shard_map/ppermute | solution.py:24
  179.4 1.7 fusion.20
  (29 shorter events, 3.9 us)
Async XLA Ops:
  6.5 120.6 %copy-start = (bf16[1,2560,640]{2,1,0:T(8,128)(2,1)S(1)}, bf16[1,2560,640]{2,1,0:T(8,128)(2,1)}, u32[]{:S(2)}) copy-start(bf16[1,2560,640]{2,1,0:T(8,128)(2,1)} %param.15) | copy-start | bytes 9830404
  6.5 5.0 %copy-start.3 = (f32[1,2560]{1,0:T(1,128)S(1)}, f32[1,2560]{1,0:T(1,128)}, u32[]{:S(2)}) copy-start(f32[1,2560]{1,0:T(1,128)} %param.17) | copy-start | bytes 30724
  6.5 56.9 %all-gather.11.cloned.1.call-start = ((), (), s32[]{:S(2)}) async-start(), calls=%async_computation.1 | async-start | bytes 1638400 | tf_op jit(solution)/shard_map/all_gather | solution.py:52
  7.3 90.8 %all-gather.13.cloned.1.call-start = ((), (), s32[]{:S(2)}) async-start(), calls=%async_computation.2 | async-start | bytes 4096000 | tf_op jit(solution)/shard_map/all_gather | solution.py:54
  8.0 154.4 %reduce-scatter.4.cloned.1.call-start = ((), (), s32[]{:S(2)}) async-start(), calls=%async_computation.3 | async-start | bytes 1638400
  32.4 13.4 %copy-start.1 = (f32[5,512,128]{2,1,0:T(8,128)}, f32[5,512,128]{2,1,0:T(8,128)S(1)}, u32[]{:S(2)}) copy-start(f32[5,512,128]{2,1,0:T(8,128)S(1)} %get-tuple-element.157) | copy-start | bytes 3932164
  137.3 32.0 %copy-start.2 = (bf16[128,640]{1,0:T(8,128)(2,1)S(1)}, bf16[128,640]{1,0:T(8,128)(2,1)}, u32[]{:S(2)}) copy-start(bf16[128,640]{1,0:T(8,128)(2,1)} %param.12) | copy-start | bytes 491524
  167.9 11.5 %collective-permute-start = (bf16[2,128,640]{2,1,0:T(8,128)(2,1)}, bf16[2,128,640]{2,1,0:T(8,128)(2,1)}, u32[]{:S(2)}, u32[]{:S(2)}) collective-permute-start(bf16[2,128,640]{2,1,0:T(8,128)(2,1)} %fusion.15), channel_id=1, source_target_pairs={{16,0},{17,1},{18,2},{19,3},{20,4},{21,5},{22,6},{23,7},{24,8},{25... | collective-permute-start | bytes 983048 | tf_op jit(solution)/shard_map/ppermute | solution.py:24
Sparse Core Ops, SparseCore 0:
  8.9 20.8 all-gather.10
  31.4 66.6 all-gather.12
  137.4 24.9 reduce-scatter.3
where the time goes:
time: 188 us
  waiting for transfers between devices  71.2 us (38%)
  blocking collectives  64.3 us (34%)
  local copies, waits for them, and re-layouts  17.4 us (9%)
  between operations  13.9 us (7%)
  matrix products  10.1 us (5%)
  other arithmetic  9.44 us (5%)
    all_gather x1, waiting for transfers between devices, body(): out_full = lax.all_gather(out_weight[0], 'tok', axis=0, tiled=True)  34.6 us
    all_gather x2, blocking collectives, combined_all(): gathered = jax.tree.map(lambda a: lax.all_gather(a, axis), part)  27.5 us
    unnamed x4, waiting for transfers between devices  26.5 us
    all_gather x1, blocking collectives, body(): query_all = lax.all_gather(saved_queries[0], 'tok', axis=0, tiled=True)  19.1 us
    all_gather x1, blocking collectives, body(): grad_all = lax.all_gather(normal_grad, 'tok', axis=0, tiled=True)  17.6 us
    unnamed x14, local copies, waits for them, and re-layouts  13.3 us
    ppermute x1, waiting for transfers between devices, shifted(): lax.ppermute(value, axis, [(source, source + steps) for source in range(l...  10.1 us
  transfers between devices with their start and end apart: 4, of which 3 were waited for; matrix products, arithmetic and copies ran while one was open for 4% of the time, Pallas kernels for 0%

commit v1 on v0

--- a/solution.py
+++ b/solution.py
@@ -5,6 +5,18 @@
 
 HD = 128
 GUIDE = 3.0
+
+
+def summed_around(x, axis, dim, contribution):
+    size, index, extent = (lax.axis_size(axis), lax.axis_index(axis), x.shape[dim])
+    upward = [(i, (i + 1) % size) for i in range(size)]
+    held, so_far = (x, None)
+    for hop in range(size):
+        coming = lax.ppermute(held, axis, upward) if hop < size - 1 else None
+        take_in = contribution(held, (index - hop) % size * extent)
+        so_far = take_in if so_far is None else so_far + take_in
+        held = coming
+    return so_far
 
 
 def combined_all(part, axis, combine):
@@ -51,9 +63,16 @@
     gate_row = block_gate[0] + time_row
     whole_cot = lax.all_gather(held_cotangents[0], "head", axis=2, tiled=True)
     scaled = (whole_cot.astype(jnp.float32) * gate_row).astype(jnp.bfloat16)
-    out_full = lax.all_gather(out_weight[0], "tok", axis=0, tiled=True)
-    attn_grad = jnp.einsum(
-        "btd,dk->btk", scaled, out_full, preferred_element_type=jnp.float32
+    attn_grad = summed_around(
+        out_weight[0],
+        "tok",
+        0,
+        lambda own_block, at: jnp.einsum(
+            "btd,dk->btk",
+            lax.dynamic_slice_in_dim(scaled, at, own_block.shape[0], axis=2),
+            own_block,
+            preferred_element_type=jnp.float32,
+        ),
     ).astype(jnp.bfloat16)
     rows_here = saved_queries.shape[1]
     groups_here = saved_queries.shape[2] // HD

time: 188 us -> 198 us (1.053)
  blocking collectives: 64.3 us -> 74.1 us
  waiting for transfers between devices: 71.2 us -> 62.7 us
  starting transfers between devices: 1.36 us -> 4.49 us
  matrix products: 10.1 us -> 13 us
    all_gather x1 -> x0, waiting for transfers between devices: 34.6 us -> none  [body(): out_full = lax.all_gather(out_weight[0], 'tok', axis=0, tiled=True)]
    ppermute x0 -> x3, waiting for transfers between devices: none -> 26.9 us  [summed_around(): coming = lax.ppermute(held, axis, upward) if hop < size - 1 else None]
    all_gather x1, blocking collectives: 19.1 us -> 31.7 us  [body(): query_all = lax.all_gather(saved_queries[0], 'tok', axis=0, tiled=True)]
    ppermute x0 -> x3, starting transfers between devices: none -> 3.17 us  [summed_around(): coming = lax.ppermute(held, axis, upward) if hop < size - 1 else None]
    dot_general x1 -> x4, matrix products: 3.51 us -> 5.27 us  [body(): jnp.einsum('btd,dk->btk', lax.dynamic_slice_in_dim(scaled, at, own_block....]
    unnamed x4 -> x3, waiting for transfers between devices: 26.5 us -> 25.7 us
    unnamed x14 -> x16, local copies, waits for them, and re-layouts: 13.3 us -> 13.8 us
  transfers between devices with their start and end apart: 4 -> 6, of which waited for: 3 -> 4; matrix products, arithmetic and copies ran while one was open for 4% -> 7% of each run, Pallas kernels for 0% -> 0%
where the time goes in v1:
time: 198 us
  blocking collectives  74.1 us (37%)
  waiting for transfers between devices  62.7 us (32%)
  local copies, waits for them, and re-layouts  17.8 us (9%)
  between operations  14.3 us (7%)
  matrix products  13 us (7%)
  other arithmetic  11 us (6%)
  starting transfers between devices  4.49 us (2%)
    all_gather x1, blocking collectives, body(): query_all = lax.all_gather(saved_queries[0], 'tok', axis=0, tiled=True)  31.7 us
    ppermute x3, waiting for transfers between devices, summed_around(): coming = lax.ppermute(held, axis, upward) if hop < size - 1 else None  26.9 us
    all_gather x2, blocking collectives, combined_all(): gathered = jax.tree.map(lambda a: lax.all_gather(a, axis), part)  26.5 us
    unnamed x3, waiting for transfers between devices  25.7 us
    all_gather x1, blocking collectives, body(): grad_all = lax.all_gather(normal_grad, 'tok', axis=0, tiled=True)  16 us
    unnamed x16, local copies, waits for them, and re-layouts  13.8 us
    ppermute x1, waiting for transfers between devices, shifted(): lax.ppermute(value, axis, [(source, source + steps) for source in range(l...  10.1 us
    dot_general x4, matrix products, body(): jnp.einsum('btd,dk->btk', lax.dynamic_slice_in_dim(scaled, at, own_block....  5.27 us
  transfers between devices with their start and end apart: 6, of which 4 were waited for; matrix products, arithmetic and copies ran while one was open for 7% of the time, Pallas kernels for 0%

profile of v1, /device:TPU:0, one launch (start us, length us, event | category | flops | bytes accessed | tf_op | source)
XLA Modules:
  0.0 197.6 jit_solution(10782131385652167420)
XLA Ops:
  7.3 3.1 %collective-permute-start = (bf16[640,640]{1,0:T(8,128)(2,1)}, bf16[640,640]{1,0:T(8,128)(2,1)}, u32[]{:S(2)}, u32[]{:S(2)}) collective-permute-start(bf16[640,640]{1,0:T(8,128)(2,1)} %bitcast.70), channel_id=1, source_target_pairs={{0,1},{1,2},{2,3},{3,0},{4,5},{5,6},{6,7},{7,4},{8,9},{9,10},{10,1... | collective-permute-start | bytes 2457608 | tf_op jit(solution)/shard_map/ppermute | solution.py:15
  11.5 31.7 %all-gather.2 = bf16[1,512,640]{1,2,0:T(8,128)(2,1)} all-gather(bf16[1,128,640]{1,2,0:T(8,128)(2,1)S(1)} %copy.22), channel_id=4, replica_groups=mesh['section'=2,'head'=4,'tok'=4] {'tok'}, dimensions={1}, use_global_device_ids=true | all-gather | bytes 819200 | tf_op jit(solution)/shard_map/all_gather | solution.py:81
  44.3 1.7 fusion.32
  47.9 13.1 %all-gather.5 = f32[4,5,512]{2,1,0:T(8,128)S(1)} all-gather(f32[1,5,512]{2,1,0:T(8,128)S(1)} %bitcast.73), channel_id=5, replica_groups=mesh['section'=2,'head'=4,'tok'=4] {'tok'}, dimensions={0}, use_global_device_ids=true | all-gather | bytes 51200 | tf_op jit(solution)/shard_map/all_gather | solution.py:23
  61.0 13.3 %all-gather.6 = f32[4,5,512]{2,1,0:T(8,128)S(1)} all-gather(f32[1,5,512]{2,1,0:T(8,128)S(1)} %bitcast.74), channel_id=6, replica_groups=mesh['section'=2,'head'=4,'tok'=4] {'tok'}, dimensions={0}, use_global_device_ids=true | all-gather | bytes 51200 | tf_op jit(solution)/shard_map/all_gather | solution.py:23
  76.5 2.6 %exponential_convert_fusion = bf16[5,512,128]{2,1,0:T(8,128)(2,1)} fusion(f32[5,512,128]{2,1,0:T(8,128)} %copy-done.1, f32[5,512]{1,0:T(8,128)S(1)} %log_add_fusion), kind=kLoop, calls=%fused_computation.12 | loop fusion | flops 655360 | bytes 1976320 | tf_op jit(solution)/shard_map/convert_element_type | solution.py:98
  79.1 14.5 %collective-permute-done.1 = bf16[640,640]{1,0:T(8,128)(2,1)} collective-permute-done((bf16[640,640]{1,0:T(8,128)(2,1)}, bf16[640,640]{1,0:T(8,128)(2,1)}, u32[]{:S(2)}, u32[]{:S(2)}) %collective-permute-start.1) | collective-permute-done | bytes 819232 | tf_op jit(solution)/shard_map/ppermute | solution.py:15
  93.6 1.6 fusion.3
  95.7 1.6 convolution_add_fusion.2
  97.3 1.6 convolution_add_fusion.1
  98.9 12.4 %collective-permute-done.2 = bf16[640,640]{1,0:T(8,128)(2,1)} collective-permute-done((bf16[640,640]{1,0:T(8,128)(2,1)}, bf16[640,640]{1,0:T(8,128)(2,1)}, u32[]{:S(2)}, u32[]{:S(2)}) %collective-permute-start.2) | collective-permute-done | bytes 819232 | tf_op jit(solution)/shard_map/ppermute | solution.py:15
  111.2 1.6 fusion.5
  113.5 16.0 %all-gather.1 = bf16[1,512,640]{2,1,0:T(8,128)(2,1)} all-gather(bf16[1,128,640]{2,1,0:T(8,128)(2,1)S(1)} %get-tuple-element.152), channel_id=3, replica_groups=mesh['section'=2,'head'=4,'tok'=4] {'tok'}, dimensions={1}, use_global_device_ids=true | all-gather | bytes 819200 | tf_op jit(solution)/shard_map/all_gather | solution.py:99
  129.5 2.5 %reshape.63 = bf16[4,128,5,128]{3,2,1,0:T(8,128)(2,1)} reshape(bf16[1,512,640]{2,1,0:T(8,128)(2,1)} %all-gather.1) | data formatting | bytes 1310720 | tf_op jit(solution)/shard_map/reshape | solution.py:103
  132.1 2.7 %fusion.4 = bf16[4,128,5,128]{1,3,2,0:T(8,128)(2,1)} fusion(bf16[4,128,5,128]{3,2,1,0:T(8,128)(2,1)} %reshape.63, bf16[5,4,128,128]{3,2,1,0:T(8,128)(2,1)} %bitcast.68), kind=kOutput, calls=%fused_computation.14 | convolution fusion | flops 84213760 | bytes 1966080 | tf_op jit(solution)/shard_map/hbij,bihe->bjhe/dot_general | solution.py:100
  136.8 3.3 %convolution_convert_fusion = bf16[2,128,2560]{2,1,0:T(8,128)(2,1)} fusion(bf16[1,2560,640]{2,1,0:T(8,128)(2,1)S(1)} %copy-done, bf16[1,128,640]{2,1,0:T(8,128)(2,1)} %get-tuple-element.153, bf16[1,128,640]{2,1,0:T(8,128)(2,1)} %copy.28), kind=kOutput, calls=%fused_computation.5 | convolution fusion | flops 839680000 | bytes 4915200 | tf_op jit(solution)/shard_map/btk,dk->btd/dot_general | solution.py:113
  140.1 4.3 %copy.33 = bf16[2,128,2560]{1,0,2:T(2,128)(2,1)} copy(bf16[2,128,2560]{2,1,0:T(8,128)(2,1)} %convolution_convert_fusion) | data formatting | bytes 2621440
  144.3 2.5 %copy.41 = bf16[320,8,2,128]{3,1,2,0:T(8,128)(2,1)} copy(bf16[320,8,2,128]{3,2,1,0:T(2,128)(2,1)} %bitcast.66) | data formatting | bytes 2621440
  146.9 25.0 %reduce-scatter.4.cloned.1.call-done = bf16[640,256]{1,0:T(8,128)(2,1)} async-done(((bf16[2560,256]{1,0:T(8,128)(2,1)}), bf16[640,256]{1,0:T(8,128)(2,1)}) %reduce-scatter.4.cloned.1.call-update) | async-done | bytes 327696
  171.9 1.8 reshape.65
  173.7 1.9 copy.34
  175.6 1.9 fusion.11
  178.9 10.1 %collective-permute-done.3 = bf16[2,128,640]{2,1,0:T(8,128)(2,1)} collective-permute-done((bf16[2,128,640]{2,1,0:T(8,128)(2,1)}, bf16[2,128,640]{2,1,0:T(8,128)(2,1)}, u32[]{:S(2)}, u32[]{:S(2)}) %collective-permute-start.3) | collective-permute-done | bytes 327712 | tf_op jit(solution)/shard_map/ppermute | solution.py:36
  189.0 1.7 fusion.16
  (38 shorter events, 10.7 us)
Async XLA Ops:
  6.5 130.3 %copy-start = (bf16[1,2560,640]{2,1,0:T(8,128)(2,1)S(1)}, bf16[1,2560,640]{2,1,0:T(8,128)(2,1)}, u32[]{:S(2)}) copy-start(bf16[1,2560,640]{2,1,0:T(8,128)(2,1)} %param.15) | copy-start | bytes 9830404
  6.5 87.0 %all-gather.9.cloned.1.call-start = ((), (), s32[]{:S(2)}) async-start(), calls=%async_computation.1 | async-start | bytes 1638400 | tf_op jit(solution)/shard_map/all_gather | solution.py:64
  7.3 164.7 %reduce-scatter.4.cloned.1.call-start = ((), (), s32[]{:S(2)}) async-start(), calls=%async_computation.2 | async-start | bytes 1638400
  7.3 67.0 %collective-permute-start = (bf16[640,640]{1,0:T(8,128)(2,1)}, bf16[640,640]{1,0:T(8,128)(2,1)}, u32[]{:S(2)}, u32[]{:S(2)}) collective-permute-start(bf16[640,640]{1,0:T(8,128)(2,1)} %bitcast.70), channel_id=1, source_target_pairs={{0,1},{1,2},{2,3},{3,0},{4,5},{5,6},{6,7},{7,4},{8,9},{9,10},{10,1... | collective-permute-start | bytes 2457608 | tf_op jit(solution)/shard_map/ppermute | solution.py:15
  46.0 1.1 copy-start.1
  46.0 29.3 %copy-start.4 = (f32[1,2560]{1,0:T(1,128)S(1)}, f32[1,2560]{1,0:T(1,128)}, u32[]{:S(2)}) copy-start(f32[1,2560]{1,0:T(1,128)} %param.17) | copy-start | bytes 30724
  74.3 19.2 %collective-permute-start.1 = (bf16[640,640]{1,0:T(8,128)(2,1)}, bf16[640,640]{1,0:T(8,128)(2,1)}, u32[]{:S(2)}, u32[]{:S(2)}) collective-permute-start(bf16[640,640]{1,0:T(8,128)(2,1)} %collective-permute-done), channel_id=1, source_target_pairs={{0,1},{1,2},{2,3},{3,0},{4,5},{5,6},{6,7},{7,4},{8,9},{9,10},{10,1... | collective-permute-start | bytes 2457608 | tf_op jit(solution)/shard_map/ppermute | solution.py:15
  93.6 17.7 %collective-permute-start.2 = (bf16[640,640]{1,0:T(8,128)(2,1)}, bf16[640,640]{1,0:T(8,128)(2,1)}, u32[]{:S(2)}, u32[]{:S(2)}) collective-permute-start(bf16[640,640]{1,0:T(8,128)(2,1)} %collective-permute-done.1), channel_id=1, source_target_pairs={{0,1},{1,2},{2,3},{3,0},{4,5},{5,6},{6,7},{7,4},{8,9},{9,10},{10,1... | collective-permute-start | bytes 2457608 | tf_op jit(solution)/shard_map/ppermute | solution.py:15
  93.6 1.6 copy-start.2
  146.9 31.9 %copy-start.3 = (bf16[128,640]{1,0:T(8,128)(2,1)S(1)}, bf16[128,640]{1,0:T(8,128)(2,1)}, u32[]{:S(2)}) copy-start(bf16[128,640]{1,0:T(8,128)(2,1)} %param.12) | copy-start | bytes 491524
  177.5 11.5 %collective-permute-start.3 = (bf16[2,128,640]{2,1,0:T(8,128)(2,1)}, bf16[2,128,640]{2,1,0:T(8,128)(2,1)}, u32[]{:S(2)}, u32[]{:S(2)}) collective-permute-start(bf16[2,128,640]{2,1,0:T(8,128)(2,1)} %fusion.11), channel_id=1, source_target_pairs={{16,0},{17,1},{18,2},{19,3},{20,4},{21,5},{22,6},{23,7},{24,8},{25... | collective-permute-start | bytes 983048 | tf_op jit(solution)/shard_map/ppermute | solution.py:36
Sparse Core Ops, SparseCore 0:
  8.9 20.8 all-gather.8
  147.0 24.8 reduce-scatter.3
